TPU v7x, 32 devices: a whole 2x2x4 slice. The times are simulated.
32 devices in a mesh: stick: 2 (over x), band: 16 (over z, y, core).
Axes of the slice: x: 2, y: 2, z: 4, core: 2. Of those that a mesh axis runs over, the one named last changes fastest.
Arguments:
- orbital_sticks: bfloat16 [32, 6144, 128], P('band', 'stick'), may hold values from -5 to 5
- stick_perm: int32 [4096], replicated, may hold values from 0 to 4095, each once
- stick_counts: int32 [2], replicated, may hold values from 1 to 3072, 4096 in all
- source_ids: int32 [1], replicated, may hold values from 0 to 31
Outputs:
- exchange: bfloat16 [32, 64, 64, 128], P(('band', 'stick'))
All inputs are finite; a program needn't handle non-finite values.
Results may differ from a plain program's by a relative error of at most 0.001.
Values may be sent and summed in bfloat16 or wider, within the bound.
A program may use at most 64 MiB of HBM per device.

v0:
```python
import math

import jax
import jax.numpy as jnp
from jax import lax
from jax.sharding import PartitionSpec as P

NX = 64
NY = 64
NZ = 128


screen_omega = 0.25


def broadcast(array, axis, root):
    mine = lax.axis_index(axis) == root
    return lax.psum(jnp.where(mine, array, jnp.zeros_like(array)), axis)


def slot_targets(stick_perm, stick_counts, capacity, slot_total):
    slots = jnp.arange(slot_total, dtype=jnp.int32)
    holder = slots // capacity
    within = slots % capacity
    offsets = jnp.cumsum(stick_counts) - stick_counts
    valid = within < stick_counts[holder]
    position = jnp.clip(offsets[holder] + within, 0, NX * NY - 1)
    return jnp.where(valid, stick_perm[position], NX * NY)


def place_sticks(blocks, targets):
    empty = jnp.zeros((blocks.shape[0], NX * NY + 1, NZ), blocks.dtype)
    filled = empty.at[:, targets].set(blocks)
    return filled[:, : NX * NY].reshape(blocks.shape[0], NX, NY, NZ)


def signed_freq(length):
    steps = jnp.arange(length, dtype=jnp.int32)
    signed = jnp.where(steps <= length // 2, steps, steps - length)
    return signed.astype(jnp.float32) / length


def screened(freq_x, freq_y, freq_z):
    square = (2.0 * math.pi) ** 2 * (
        freq_x[:, None, None] ** 2 + freq_y[None, :, None] ** 2 + freq_z[None, None, :] ** 2
    )
    safe = jnp.where(square > 0, square, 1.0)
    inner = 4.0 * math.pi * (1.0 - jnp.exp(-square / (4.0 * screen_omega**2))) / safe
    return jnp.where(square > 0, inner, math.pi / screen_omega**2)


def hartley_table(length):
    steps = jnp.arange(length, dtype=jnp.int32)
    product = steps[:, None] * steps[None, :] % length
    angle = product.astype(jnp.float32) * (2.0 * math.pi / length)
    return jnp.cos(angle) + jnp.sin(angle)


def hartley(field, table_x, table_y, table_z):
    highest = lax.Precision.HIGHEST
    section = jnp.einsum("bxyz,zc->bxyc", field, table_z, precision=highest)
    section = jnp.einsum("bxyc,yd->bxdc", section, table_y, precision=highest)
    return jnp.einsum("bxdc,xe->bedc", section, table_x, precision=highest)


def local(orbital_sticks, stick_perm, stick_counts, source_ids):
    stick_total = lax.axis_size("stick")
    rows, capacity, depth = orbital_sticks.shape
    targets = slot_targets(stick_perm, stick_counts, capacity, stick_total * capacity)
    regrouped = lax.all_to_all(orbital_sticks, "stick", split_axis=0, concat_axis=1, tiled=True)
    owned = place_sticks(regrouped, targets)
    table_x = hartley_table(NX)
    table_y = hartley_table(NY)
    table_z = hartley_table(NZ)
    kernel = screened(signed_freq(NX), signed_freq(NY), signed_freq(NZ))
    orbital_id = source_ids[0]
    group = orbital_id // rows
    local_row = orbital_id % rows
    piece = lax.dynamic_index_in_dim(orbital_sticks, local_row, 0, keepdims=False)
    piece = broadcast(piece, "band", group)
    blocks = lax.all_gather(piece, "stick", axis=0, tiled=True)
    source = place_sticks(blocks[None], targets)[0]
    source_value = source.astype(jnp.float32)[None]
    density = owned.astype(jnp.float32) * source_value
    spectrum = hartley(density, table_x, table_y, table_z) * kernel[None]
    potential = hartley(spectrum, table_x, table_y, table_z) / (NX * NY * NZ)
    total = source_value * potential
    return (-total).astype(jnp.bfloat16)


def solution(mesh):
    placed = (P("band", "stick", None), P(), P(), P())
    return jax.shard_map(
        local,
        mesh=mesh,
        in_specs=placed,
        out_specs=P(("band", "stick"), None, None, None),
        check_vma=False,
    )
```

profile of v0, /device:TPU:5, one launch (start us, length us, event | category | flops | bytes accessed | tf_op | source)
XLA Modules:
  0.0 204.1 jit_solution(2869489448109365349)
XLA Ops:
  6.5 0.0 copy-start
  6.5 0.0 copy-start.1
  6.5 0.0 copy-start.3
  6.5 3.8 %all-to-all-start = ((bf16[2,3072,128]{2,1,0:T(8,128)(2,1)}), bf16[2,3072,128]{2,1,0:T(8,128)(2,1)S(1)}, u32[]{:S(2)}, u32[]{:S(2)}) async-start(bf16[2,3072,128]{2,1,0:T(8,128)(2,1)} %param.4), calls=%async_computation | async-start | bytes 3145728 | tf_op jit(solution)/shard_map/all_to_all | solution.py:70
  10.4 0.0 all-reduce.2.cloned.1.call-start
  11.1 0.0 copy-done.1
  11.1 0.9 select_bitcast_fusion
  12.0 0.0 all-reduce.2.cloned.1.call-update
  12.1 0.0 all-gather.2.cloned.1.call-start
  12.1 0.0 copy-done.3
  12.1 0.2 reduce-window.9
  12.3 0.6 fusion.85
  12.9 1.3 compare_select_fusion.3
  14.2 0.7 fusion.84
  14.9 92.5 %all-reduce.2.cloned.1.call-done = bf16[3072,128]{1,0:T(8,128)(2,1)} async-done(((bf16[3072,128]{1,0:T(8,128)(2,1)}), bf16[3072,128]{1,0:T(8,128)(2,1)}) %all-reduce.2.cloned.1.call-update) | async-done | bytes 786448 | tf_op jit(solution)/shard_map/psum | solution.py:18
  107.4 0.0 all-gather.2.cloned.1.call-update
  107.4 0.0 copy-done
  107.4 34.3 %gather_fusion = s32[6144]{0:T(1024)S(1)} fusion(s32[4096]{0:T(1024)S(1)} %copy-done, s32[6144]{0:T(1024)S(1)} %broadcast_clamp_fusion), kind=kCustom, calls=%fused_computation | custom fusion | bytes 73728 | tf_op jit(solution)/shard_map/gather | solution.py:28
  141.7 0.1 broadcast_add_fusion
  141.8 1.5 compare_select_fusion.2
  143.3 0.0 all-to-all-done
  143.3 0.0 copy-start.2
  143.3 1.1 copy-done.2
  144.4 16.5 %scatter_custom_fusion.1 = bf16[4097,128]{1,0:T(8,128)(2,1)S(1)} fusion(s32[6144]{0:T(1024)S(1)} %bitcast.64, bf16[6144,128]{1,0:T(8,128)(2,1)} %bitcast.61, bf16[]{:T(256)} %constant.104.clone.1), kind=kCustom, calls=%fused_computation.29 | custom fusion | bytes 1049344 | tf_op jit(solution)/shard_map/scatter | solution.py:33
  160.9 0.1 slice.17
  161.0 0.0 all-gather.2.cloned.1.call-done
  161.0 16.7 %scatter_custom_fusion = bf16[4097,128]{1,0:T(8,128)(2,1)S(1)} fusion(s32[6144]{0:T(1024)S(1)} %bitcast.65, bf16[6144,128]{1,0:T(8,128)(2,1)} %all-gather.2.cloned.1.call-done, bf16[]{:T(256)} %constant.104.clone.1), kind=kCustom, calls=%fused_computation.31 | custom fusion | bytes 1049344 | tf_op jit(solution)/shard_map/scatter | solution.py:33
  177.7 0.1 slice.16
  177.8 0.2 convert.2
  178.0 2.1 %fusion.2 = f32[64,64,128]{2,1,0:T(8,128)S(1)} fusion(bf16[64,64,128]{2,1,0:T(8,128)(2,1)S(1)} %bitcast.60, bf16[64,64,128]{2,1,0:T(8,128)(2,1)S(1)} %bitcast.57), kind=kOutput, calls=%fused_computation.8 | convolution fusion | flops 807124992 | bytes 4194304 | tf_op jit(solution)/shard_map/bxyz,zc->bxyc/dot_general | solution.py:61
  180.1 2.1 %convolution_bitcast_fusion.1 = f32[64,64,128]{2,1,0:T(8,128)S(1)} fusion(f32[64,64,128]{2,1,0:T(8,128)S(1)} %fusion.2), kind=kOutput, calls=%fused_computation.18 | convolution fusion | flops 402714624 | bytes 4194304 | tf_op jit(solution)/shard_map/bxyc,yd->bxdc/dot_general | solution.py:62
  182.2 3.1 %fusion.3 = f32[64,64,128]{2,0,1:T(8,128)S(1)} fusion(f32[64,64,128]{2,1,0:T(8,128)S(1)} %convolution_bitcast_fusion.1), kind=kOutput, calls=%fused_computation.9 | convolution fusion | flops 402714624 | bytes 4194304 | tf_op jit(solution)/shard_map/bxdc,xe->bedc/dot_general | solution.py:63
  185.3 3.7 %fusion.9 = f32[64,64,128]{2,1,0:T(8,128)S(1)} fusion(f32[64,64,128]{2,0,1:T(8,128)S(1)} %fusion.3, f32[128]{0:T(128)S(1)} %fusion.53, f32[64,64]{1,0:T(8,128)S(1)} %broadcast_add_fusion), kind=kOutput, calls=%fused_computation.16 | convolution fusion | flops 811319296 | bytes 4211200 | tf_op jit(solution)/shard_map/bxyz,zc->bxyc/dot_general | solution.py:61
  189.0 2.3 %convolution_bitcast_fusion = f32[64,64,128]{2,1,0:T(8,128)S(1)} fusion(f32[64,64,128]{2,1,0:T(8,128)S(1)} %fusion.9), kind=kOutput, calls=%fused_computation.17 | convolution fusion | flops 402714624 | bytes 4194304 | tf_op jit(solution)/shard_map/bxyc,yd->bxdc/dot_general | solution.py:62
  191.3 4.3 %fusion.13 = bf16[1,64,64,128]{3,1,2,0:T(8,128)(2,1)S(1)} fusion(f32[64,64,128]{2,1,0:T(8,128)S(1)} %convolution_bitcast_fusion, f32[64,64,128]{2,1,0:T(8,128)S(1)} %convert.2), kind=kOutput, calls=%fused_computation.19 | convolution fusion | flops 404811776 | bytes 5242880 | tf_op jit(solution)/shard_map/bxdc,xe->bedc/dot_general | solution.py:63
  195.6 1.6 copy.9
  (4 shorter events, 0.0 us)
Async XLA Ops:
  6.5 100.9 %copy-start = (s32[4096]{0:T(1024)S(1)}, s32[4096]{0:T(1024)}, u32[]{:S(2)}) copy-start(s32[4096]{0:T(1024)} %param.5) | copy-start | bytes 49156
  6.5 4.5 %copy-start.1 = (bf16[2,3072,128]{2,1,0:T(8,128)(2,1)S(1)}, bf16[2,3072,128]{2,1,0:T(8,128)(2,1)}, u32[]{:S(2)}) copy-start(bf16[2,3072,128]{2,1,0:T(8,128)(2,1)} %param.4) | copy-start | bytes 4718596
  6.5 5.6 %copy-start.3 = (s32[2]{0:T(128)S(1)}, s32[2]{0:T(128)}, u32[]{:S(2)}) copy-start(s32[2]{0:T(128)} %param.6) | copy-start | bytes 28
  6.5 136.7 %all-to-all-start = ((bf16[2,3072,128]{2,1,0:T(8,128)(2,1)}), bf16[2,3072,128]{2,1,0:T(8,128)(2,1)S(1)}, u32[]{:S(2)}, u32[]{:S(2)}) async-start(bf16[2,3072,128]{2,1,0:T(8,128)(2,1)} %param.4), calls=%async_computation | async-start | bytes 3145728 | tf_op jit(solution)/shard_map/all_to_all | solution.py:70
  10.4 97.0 %all-reduce.2.cloned.1.call-start = ((), (), s32[]{:S(2)}) async-start(), calls=%async_computation.1 | async-start | bytes 1572864 | tf_op jit(solution)/shard_map/psum | solution.py:18
  12.1 149.0 %all-gather.2.cloned.1.call-start = ((), (), s32[]{:S(2)}) async-start(), calls=%async_computation.2 | async-start | bytes 2359296 | tf_op jit(solution)/shard_map/all_gather | solution.py:81
  143.3 1.2 copy-start.2
Sparse Core Ops, SparseCore 0:
  14.6 92.7 all-reduce.1
  108.9 27.7 all-gather.1
where the time goes:
time: 208 us; the launch traced here: 204 us
  waiting for transfers between devices  92.5 us (44%)
  local copies, waits for them, and re-layouts  71.7 us (34%)
  matrix products  17.5 us (8%)
  between operations  14.3 us (7%)
  other arithmetic  4.23 us (2%)
  starting transfers between devices  3.89 us (2%)
    psum x1, waiting for transfers between devices, broadcast(): return lax.psum(jnp.where(mine, array, jnp.zeros_like(array)), axis)  92.5 us
    gather x1, local copies, waits for them, and re-layouts, slot_targets(): return jnp.where(valid, stick_perm[position], NX * NY)  34.3 us
    scatter x2, local copies, waits for them, and re-layouts, place_sticks(): filled = empty.at[:, targets].set(blocks)  33.2 us
    dot_general x2, matrix products, hartley(): return jnp.einsum('bxdc,xe->bedc', section, table_x, precision=highest)  7.35 us
    dot_general x2, matrix products, hartley(): section = jnp.einsum('bxyz,zc->bxyc', field, table_z, precision=highest)  5.73 us
    dot_general x2, matrix products, hartley(): section = jnp.einsum('bxyc,yd->bxdc', section, table_y, precision=highest)  4.45 us
  transfers between devices with their start and end apart: 3, of which 1 were waited for; matrix products, arithmetic and copies ran while one was open for 27% of the time, Pallas kernels for 0%

commit v1 on v0

v1 whole, which is shorter than its diff:
```python
import functools
import math

import jax
import jax.numpy as jnp
import numpy as np
from jax import lax
from jax.experimental import pallas as pl
from jax.experimental.pallas import tpu as pltpu
from jax.sharding import PartitionSpec as P

NX = 64
NY = 64
NZ = 128
CHUNKS = 8

screen_omega = 0.25


def signed_freq(length):
    steps = np.arange(length, dtype=np.int32)
    signed = np.where(steps <= length // 2, steps, steps - length)
    return signed.astype(np.float64) / length


def screened(freq_x, freq_y, freq_z):
    square = (2.0 * math.pi) ** 2 * (
        freq_x[:, None, None] ** 2 + freq_y[None, :, None] ** 2 + freq_z[None, None, :] ** 2
    )
    safe = np.where(square > 0, square, 1.0)
    inner = 4.0 * math.pi * (1.0 - np.exp(-square / (4.0 * screen_omega**2))) / safe
    return np.where(square > 0, inner, math.pi / screen_omega**2)


def hartley_table(length):
    steps = np.arange(length, dtype=np.int64)
    angle = (steps[:, None] * steps[None, :] % length) * (2.0 * math.pi / length)
    return np.cos(angle) + np.sin(angle)


def halves(table):
    high = table.astype(jnp.bfloat16)
    low = (table - high.astype(np.float64)).astype(jnp.bfloat16)
    return high, low


def band_shape(bands):
    return (bands // 4, 2, 2) if bands % 4 == 0 else (bands, 1, 1)


def spread_kernel(root, sticks, shape, chunk, piece, mine, source, owned, local_sem, tree_send, tree_recv,
                  peer_send, peer_recv, core_send, core_recv, swap_send, swap_recv):
    lines, wide, cores = shape
    stick = lax.axis_index("stick")
    band = lax.axis_index("band")
    core = band % cores
    row = (band // cores) % wide
    line = band // (cores * wide)
    root_core = root % cores
    root_row = (root // cores) % wide
    root_line = root // (cores * wide)
    place = lambda l, r, c: (l * wide + r) * cores + c

    barrier = pltpu.get_barrier_semaphore()

    def greet(**where):
        pl.semaphore_signal(barrier, inc=1, device_id=where, device_id_type=pl.DeviceIdType.MESH)

    pl.when(line > 0)(lambda: greet(band=place(line - 1, row, core)))
    pl.when(line < lines - 1)(lambda: greet(band=place(line + 1, row, core)))
    for step in range(1, wide):
        greet(band=place(line, (row + step) % wide, core))
    for step in range(1, cores):
        greet(band=place(line, row, (core + step) % cores))
    for step in range(1, sticks):
        greet(stick=(stick + step) % sticks)
    near = jnp.where(line > 0, 1, 0) + jnp.where(line < lines - 1, 1, 0)
    pl.semaphore_wait(barrier, near + (wide - 1) + (cores - 1) + (sticks - 1))

    def remote(src, dst, send, recv, **where):
        return pltpu.make_async_remote_copy(
            src_ref=src, dst_ref=dst, send_sem=send, recv_sem=recv,
            device_id=where, device_id_type=pl.DeviceIdType.MESH)

    def swap(step, k):
        rows = pl.ds(pl.multiple_of(k * chunk, chunk), chunk)
        peer = (stick + step) % sticks
        return remote(mine.at[peer, rows], owned.at[stick, rows], swap_send.at[step, k], swap_recv.at[step, k],
                      stick=peer)

    keep = pltpu.make_async_copy(mine.at[stick], owned.at[stick], local_sem.at[0])
    keep.start()
    primary = core == root_core
    is_root = band == root
    held = pltpu.make_async_copy(piece, source.at[stick], local_sem.at[1])
    pl.when(is_root)(held.start)

    def tree(slot, k, target):
        rows = pl.ds(pl.multiple_of(k * chunk, chunk), chunk)
        return lambda src: remote(src.at[rows], source.at[stick, rows], tree_send.at[slot, k], tree_recv.at[k],
                                  band=target)

    up_ok = primary & (row == root_row) & (line >= root_line) & (line < lines - 1)
    down_ok = primary & (row == root_row) & (line <= root_line) & (line > 0)
    side_ok = primary & (row == root_row)
    exits = [(up_ok, place(line + 1, row, core)), (down_ok, place(line - 1, row, core))]
    exits += [(side_ok, place(line, (row + step) % wide, core)) for step in range(1, wide)]

    def fan(k, src):
        rows = pl.ds(pl.multiple_of(k * chunk, chunk), chunk)
        for slot, (allowed, target) in enumerate(exits):
            pl.when(allowed)(lambda slot=slot, target=target: tree(slot, k, target)(src).start())
        for step in range(1, sticks):
            remote(src.at[rows], source.at[stick, rows], peer_send.at[step, k], peer_recv.at[step, k],
                   stick=(stick + step) % sticks).start()
        for step in range(1, cores):
            remote(src.at[rows], source.at[stick, rows], core_send.at[step, 0, k], core_recv.at[0, k],
                   band=place(line, row, (core + step) % cores)).start()

    def tree_arrival(k):
        rows = pl.ds(pl.multiple_of(k * chunk, chunk), chunk)
        return remote(source.at[stick, rows], source.at[stick, rows], tree_send.at[0, k], tree_recv.at[k],
                      band=place(line, (row + 1) % wide, core))

    def peer_copy(step, k):
        rows = pl.ds(pl.multiple_of(k * chunk, chunk), chunk)
        peer = (stick + step) % sticks
        return peer, remote(source.at[stick, rows], source.at[stick, rows], peer_send.at[step, k],
                            peer_recv.at[step, k], stick=peer)

    def relay(k):
        rows = pl.ds(pl.multiple_of(k * chunk, chunk), chunk)
        for step in range(1, sticks):
            peer_copy(step, k)[1].wait_recv()
            sender = (stick + sticks - step) % sticks
            for other in range(1, cores):
                remote(source.at[sender, rows], source.at[sender, rows], core_send.at[other, step, k],
                       core_recv.at[step, k], band=place(line, row, (core + other) % cores)).start()

    @pl.when(primary)
    def _():
        @pl.loop(0, CHUNKS)
        def _(k):
            @pl.when(is_root)
            def _():
                fan(k, piece)

            @pl.when(jnp.logical_not(is_root))
            def _():
                tree_arrival(k).wait_recv()
                fan(k, source.at[stick])

            for step in range(1, sticks):
                swap(step, k).start()
            pl.when(k > 0)(lambda: relay(k - 1))

        relay(CHUNKS - 1)

    @pl.when(jnp.logical_not(primary))
    def _():
        @pl.loop(0, CHUNKS)
        def _(k):
            for step in range(1, sticks):
                swap(step, k).start()

        @pl.loop(0, CHUNKS)
        def _(k):
            rows = pl.ds(pl.multiple_of(k * chunk, chunk), chunk)
            for step in range(sticks):
                sender = (stick + sticks - step) % sticks
                remote(source.at[sender, rows], source.at[sender, rows], core_send.at[0, step, k],
                       core_recv.at[step, k], band=place(line, row, (core + 1) % cores)).wait_recv()

    @pl.when(primary)
    def _():
        @pl.loop(0, CHUNKS)
        def _(k):
            for slot, (allowed, target) in enumerate(exits):
                pl.when(allowed)(lambda slot=slot, target=target: tree(slot, k, target)(piece).wait_send())
            for step in range(1, sticks):
                peer_copy(step, k)[1].wait_send()
            rows = pl.ds(pl.multiple_of(k * chunk, chunk), chunk)
            for other in range(1, cores):
                for step in range(sticks):
                    sender = (stick + sticks - step) % sticks
                    remote(source.at[sender, rows], source.at[sender, rows], core_send.at[other, step, k],
                           core_recv.at[step, k], band=place(line, row, (core + other) % cores)).wait_send()

    @pl.loop(0, CHUNKS)
    def _(k):
        for step in range(1, sticks):
            swap(step, k).wait()

    pl.when(is_root)(held.wait)
    keep.wait()


def spread(root, sticks, bands, piece, mine):
    capacity, depth = piece.shape
    shape = band_shape(bands)
    lines, wide, cores = shape
    dma = pltpu.SemaphoreType.DMA
    block = jax.ShapeDtypeStruct((sticks, capacity, depth), piece.dtype)
    anywhere = pl.BlockSpec(memory_space=pl.ANY)
    return pl.pallas_call(
        functools.partial(spread_kernel, root, sticks, shape, capacity // CHUNKS),
        out_shape=(block, block),
        in_specs=[anywhere, anywhere],
        out_specs=(anywhere, anywhere),
        scratch_shapes=[
            dma((2,)),
            dma((wide + 1, CHUNKS)),
            dma((CHUNKS,)),
            dma((sticks, CHUNKS)),
            dma((sticks, CHUNKS)),
            dma((cores, sticks, CHUNKS)),
            dma((sticks, CHUNKS)),
            dma((sticks, CHUNKS)),
            dma((sticks, CHUNKS)),
        ],
        compiler_params=pltpu.CompilerParams(collective_id=root, has_side_effects=True),
    )(piece, mine)


def spread_far(group, piece, mine):
    is_root = lax.axis_index("band") == group
    piece = lax.psum(jnp.where(is_root, piece, jnp.zeros_like(piece)), "band")
    source = lax.all_gather(piece, "stick", axis=0, tiled=False)
    owned = lax.all_to_all(mine, "stick", split_axis=0, concat_axis=0, tiled=True)
    return source, owned


def split(value):
    high = value.astype(jnp.bfloat16)
    low = (value - high.astype(jnp.float32)).astype(jnp.bfloat16)
    return high, low


def left(table, value):
    high, low = split(value)
    return jnp.dot(table, jnp.concatenate([high, low, high], axis=0), preferred_element_type=jnp.float32)


def along_z(value, table):
    high, low = split(value)
    both = jnp.dot(jnp.concatenate([high, low], axis=1), table, preferred_element_type=jnp.float32)
    return both[:, :NZ] + both[:, NZ:]


def exchange_kernel(sticks, capacity, perm, counts, owned, source, table_x, table_y, table_z, kernel, out,
                    pair_slot, source_slot, grid, source_grid, turned):
    rows = 128

    @pl.loop(0, sticks * capacity // rows)
    def _(i):
        at = pl.ds(pl.multiple_of(i * rows, rows), rows)
        value = source[at, :].astype(jnp.float32)
        source_slot[at, :] = value
        pair_slot[at, :] = owned[at, :].astype(jnp.float32) * value

    offset = 0
    for block in range(sticks):
        count = counts[block]

        def move(i, first, base):
            target = perm[first + i]
            grid[pl.ds(target, 1), :] = pair_slot[pl.ds(base + i, 1), :]
            source_grid[pl.ds(target, 1), :] = source_slot[pl.ds(base + i, 1), :]

        base = block * capacity

        @pl.loop(0, count // 16)
        def _(j):
            for u in range(16):
                move(j * 16 + u, offset, base)

        @pl.loop(count // 16 * 16, count)
        def _(i):
            move(i, offset, base)

        offset = offset + count

    def two(ref, first, length):
        a = ref[pl.ds(pl.multiple_of(first * length, length), length), :]
        b = ref[pl.ds(pl.multiple_of(first * length + length, length), length), :]
        return jnp.concatenate([a, b], axis=1)

    def turn(ref, value, first, many, stride):
        ref[pl.ds(first, many, stride=stride), :] = value[:, :NZ]
        ref[pl.ds(first + 1, many, stride=stride), :] = value[:, NZ:]

    def forward_y(i, _):
        turn(turned, left(table_y[...], two(grid, 2 * i, NY)), 2 * i, NY, NX)
        return 0

    lax.fori_loop(0, NX // 2, forward_y, 0, unroll=2)

    def middle(i, _):
        value = left(table_x[...], two(turned, 2 * i, NX))
        value = jnp.concatenate([value[:, :NZ], value[:, NZ:]], axis=0)
        value = along_z(value, table_z[...])
        value = value * kernel[pl.ds(pl.multiple_of(i * 2 * NX, 2 * NX), 2 * NX), :]
        value = along_z(value, table_z[...])
        value = jnp.concatenate([value[:NX], value[NX:]], axis=1)
        turn(grid, left(table_x[...], value), 2 * i, NX, NY)
        return 0

    lax.fori_loop(0, NY // 2, middle, 0, unroll=2)

    def inverse_y(i, _):
        value = left(table_y[...], two(grid, 2 * i, NY))
        at = pl.ds(pl.multiple_of(i * 2 * NY, 2 * NY), 2 * NY)
        value = jnp.concatenate([value[:, :NZ], value[:, NZ:]], axis=0)
        out[at, :] = (value * source_grid[at, :]).astype(jnp.bfloat16)
        return 0

    lax.fori_loop(0, NX // 2, inverse_y, 0, unroll=2)


def exchange(stick_perm, stick_counts, owned, source):
    sticks, capacity, depth = owned.shape
    table_x, low_x = halves(hartley_table(NX))
    table_y, low_y = halves(hartley_table(NY))
    table_z, low_z = halves(hartley_table(NZ))
    left_x = jnp.asarray(np.concatenate([table_x, table_x, low_x], axis=1))
    left_y = jnp.asarray(np.concatenate([table_y, table_y, low_y], axis=1))
    right_z = np.concatenate(
        [np.concatenate([table_z, low_z], axis=1), np.concatenate([table_z, np.zeros_like(low_z)], axis=1)], axis=0)
    right_z = jnp.asarray(right_z)
    kernel = screened(signed_freq(NX), signed_freq(NY), signed_freq(NZ)) * (-1.0 / (NX * NY * NZ))
    kernel = jnp.asarray(kernel.transpose(1, 0, 2).reshape(NX * NY, NZ), jnp.float32)
    smem = pl.BlockSpec(memory_space=pltpu.SMEM)
    vmem = pl.BlockSpec(memory_space=pltpu.VMEM)
    slots = sticks * capacity
    full = lambda n: pltpu.VMEM((n, NZ), jnp.float32)
    return pl.pallas_call(
        functools.partial(exchange_kernel, sticks, capacity),
        out_shape=jax.ShapeDtypeStruct((NX * NY, NZ), jnp.bfloat16),
        in_specs=[smem, smem] + [vmem] * 6,
        out_specs=vmem,
        scratch_shapes=[full(slots), full(slots), full(NX * NY), full(NX * NY), full(NX * NY)],
        compiler_params=pltpu.CompilerParams(vmem_limit_bytes=40 << 20),
    )(stick_perm, stick_counts, owned.reshape(slots, depth), source.reshape(slots, depth),
      left_x, left_y, right_z, kernel)


def local(orbital_sticks, stick_perm, stick_counts, source_ids):
    sticks = lax.axis_size("stick")
    bands = lax.axis_size("band")
    rows = orbital_sticks.shape[0]
    group = source_ids[0] // rows
    piece = lax.dynamic_index_in_dim(orbital_sticks, source_ids[0] % rows, 0, keepdims=False)
    if bands <= 16:
        branches = [functools.partial(spread, root, sticks, bands) for root in range(bands)]
        source, owned = lax.switch(group, branches, piece, orbital_sticks)
    else:
        source, owned = spread_far(group, piece, orbital_sticks)
    out = exchange(stick_perm, stick_counts, owned, source)
    return out.reshape(1, NX, NY, NZ)


def solution(mesh):
    placed = (P("band", "stick", None), P(), P(), P())
    return jax.shard_map(
        local,
        mesh=mesh,
        in_specs=placed,
        out_specs=P(("band", "stick"), None, None, None),
        check_vma=False,
    )
```

time: 208 us -> 85.5 us (0.41); the launches traced: 204 us -> 85.1 us
  waiting for transfers between devices: 92.5 us -> 0 us
  Pallas kernels: 0 us -> 82.1 us
  local copies, waits for them, and re-layouts: 71.7 us -> 2.23 us
  matrix products: 17.5 us -> 0 us
  between operations: 14.3 us -> 0.77 us
  other arithmetic: 4.23 us -> 0 us
  starting transfers between devices: 3.89 us -> 0 us
    psum x1 -> x0, waiting for transfers between devices: 92.5 us -> none  [broadcast(): return lax.psum(jnp.where(mine, array, jnp.zeros_like(array)), axis)]
    pallas_call x0 -> x2, Pallas kernels: none -> 82.1 us  [the longest x1 51.3 us: spread(): pl.pallas_call(functools.partial(spread_kernel, root, sticks, shape, capa...]
    gather x3 -> x0, local copies, waits for them, and re-layouts: 35.5 us -> none  [the longest x1 34.3 us: slot_targets(): return jnp.where(valid, stick_perm[position], NX * NY)]
    scatter x2 -> x0, local copies, waits for them, and re-layouts: 33.2 us -> none  [place_sticks(): filled = empty.at[:, targets].set(blocks)]
    dot_general x6 -> x0, matrix products: 17.5 us -> none  [the longest x2 7.35 us: hartley(): return jnp.einsum('bxdc,xe->bedc', section, table_x, precision=highest)]
    all_to_all x1 -> x0, starting transfers between devices: 3.8 us -> none  [local(): lax.all_to_all(orbital_sticks, 'stick', split_axis=0, concat_axis=1, tile...]
    select_n x3 -> x0, other arithmetic: 3.72 us -> none  [the longest x1 1.45 us: place_sticks(): filled = empty.at[:, targets].set(blocks)]
    squeeze x0 -> x1, local copies, waits for them, and re-layouts: none -> 2.2 us  [local(): lax.dynamic_index_in_dim(orbital_sticks, source_ids[0] % rows, 0, keepdim...]
  transfers between devices with their start and end apart: 3 -> 0, of which waited for: 1 -> 0; matrix products, arithmetic and copies ran while one was open for 27% -> 0% of each run, Pallas kernels for 0% -> 0%
where the time goes in v1:
time: 85.5 us; the launch traced here: 85.1 us
  Pallas kernels  82.1 us (96%)
  local copies, waits for them, and re-layouts  2.23 us (3%)
    pallas_call x1, Pallas kernels, spread(): pl.pallas_call(functools.partial(spread_kernel, root, sticks, shape, capa...  51.3 us
    pallas_call x1, Pallas kernels, exchange(): pl.pallas_call(functools.partial(exchange_kernel, sticks, capacity), out_...  30.7 us
    squeeze x1, local copies, waits for them, and re-layouts, local(): lax.dynamic_index_in_dim(orbital_sticks, source_ids[0] % rows, 0, keepdim...  2.2 us

profile of v1, /device:TPU:5, one launch (start us, length us, event | category | flops | bytes accessed | tf_op | source)
XLA Modules:
  0.0 85.1 jit_solution(6493539102319815943)
XLA Ops:
  0.7 0.0 copy-start
  0.7 0.0 copy-start.1
  0.7 0.0 copy-start.2
  0.7 0.0 copy-start.3
  0.7 0.0 copy-start.4
  0.7 53.6 %conditional.1 = (bf16[6144,128]{1,0:T(8,128)(2,1)}, bf16[6144,128]{1,0:T(8,128)(2,1)}) conditional(s32[]{:T(128)} %clamp.3, (s32[]{:T(128)}, bf16[2,3072,128]{2,1,0:T(8,128)(2,1)}) %tuple.133, (s32[]{:T(128)}, bf16[2,3072,128]{2,1,0:T(8,128)(2,1)}) %tuple.133, (s32[]{:T(128)}, ...), branch_computations={%region_0.1_spmd, %region_1.2_spmd, %region_2.3_spmd, %region_3.4_... | conditional | flops 3 | bytes 1572918 | solution.py:355
  0.8 2.2 %dynamic-slice_bitcast_fusion.3.piece = bf16[3072,128]{1,0:T(8,128)(2,1)} fusion(bf16[2,3072,128]{2,1,0:T(8,128)(2,1)} %get-tuple-element.547.mine, s32[]{:T(128)S(6)} %select_n.62), kind=kLoop, calls=%fused_computation.3 | loop fusion | bytes 1572868 | tf_op jit(solution)/shard_map/jit(dynamic_index_in_dim)/squeeze | solution.py:352
  3.0 51.3 %branch_3_fun.2 = (bf16[2,3072,128]{2,1,0:T(8,128)(2,1)}, bf16[2,3072,128]{2,1,0:T(8,128)(2,1)}) custom-call(bf16[3072,128]{1,0:T(8,128)(2,1)} %dynamic-slice_bitcast_fusion.3.piece, bf16[2,3072,128]{2,1,0:T(8,128)(2,1)} %get-tuple-element.547.mine), custom_call_target="tpu_custom_call" | custom-call | tf_op jit(solution)/shard_map/cond/branch_3_fun/pallas_call | solution.py:205
  54.4 0.0 copy-done
  54.4 0.0 copy-done.1
  54.4 0.0 copy-done.2
  54.4 0.0 copy-done.3
  54.4 0.0 copy-done.4
  54.4 30.7 %shard_map.82 = bf16[4096,128]{1,0:T(8,128)(2,1)} custom-call(s32[4096]{0:T(1024)S(1)} %copy-done.3, s32[2]{0:T(128)S(1)} %copy-done.4, bf16[6144,128]{1,0:T(8,128)(2,1)} %get-tuple-element.601.owned, bf16[6144,128]{1,0:T(8,128)(2,1)} %get-tuple-element.602.source, bf16[64,192]{1,0:T(8,128)(2,1)S(1)} %copy-done.1, bf16[64,192]{1,0:T(8,128)(2,1)S(1)} %copy-done.1, ...), custom_call_target="tpu_custom_call" | custom-call | tf_op jit(solution)/shard_map/pallas_call | solution.py:336
Async XLA Ops:
  0.7 53.7 %copy-start = (f32[4096,128]{1,0:T(8,128)S(1)}, f32[4096,128]{1,0:T(8,128)}, u32[]{:S(2)}) copy-start(f32[4096,128]{1,0:T(8,128)} %constant.119.clone.kernel) | copy-start | bytes 6291460
  0.7 53.7 %copy-start.1 = (bf16[64,192]{1,0:T(8,128)(2,1)S(1)}, bf16[64,192]{1,0:T(8,128)(2,1)}, u32[]{:S(2)}) copy-start(bf16[64,192]{1,0:T(8,128)(2,1)} %constant.117.clone.table_x.table_y) | copy-start | bytes 73732
  0.7 53.7 %copy-start.2 = (bf16[256,256]{1,0:T(8,128)(2,1)S(1)}, bf16[256,256]{1,0:T(8,128)(2,1)}, u32[]{:S(2)}) copy-start(bf16[256,256]{1,0:T(8,128)(2,1)} %constant.118.clone.table_z) | copy-start | bytes 393220
  0.7 53.7 %copy-start.3 = (s32[4096]{0:T(1024)S(1)}, s32[4096]{0:T(1024)}, u32[]{:S(2)}) copy-start(s32[4096]{0:T(1024)} %perm.1) | copy-start | bytes 49156
  0.7 53.7 %copy-start.4 = (s32[2]{0:T(128)S(1)}, s32[2]{0:T(128)}, u32[]{:S(2)}) copy-start(s32[2]{0:T(128)} %counts.1) | copy-start | bytes 28
